TPU v7x, 128 devices: a whole 4x4x4 slice. The times are simulated.
128 devices in a mesh: node: 16 (over z, y), local: 8 (over x, core).
Axes of the slice: x: 4, y: 4, z: 4, core: 2. Of those that a mesh axis runs over, the one named last changes fastest.
Arguments:
- out_grad: bfloat16 [2048, 3584], P(('node', 'local')), may hold values from -6 to 6
- saved_input: bfloat16 [2048, 3584], P(('node', 'local')), may hold values from -6 to 6
- routes: int32 [2048, 8], P(('node', 'local')), may hold values from 0 to 127, as said below
- gate_int: int32 [2048, 8], P(('node', 'local')), may hold values from 4096 to 65535
- w_gate: bfloat16 [128, 3584, 1024], P(('node', 'local')), may hold values from -0.09375 to 0.09375
- w_up: bfloat16 [128, 3584, 1024], P(('node', 'local')), may hold values from -0.09375 to 0.09375
- w_down: bfloat16 [128, 1024, 3584], P(('node', 'local')), may hold values from -0.09375 to 0.09375
Outputs:
- input_grad: bfloat16 [2048, 3584], P(('node', 'local'))
- gate_grad: bfloat16 [2048, 8], P(('node', 'local'))
Inputs may be any that keep to these rules, and one draw needn't show every extreme that they name: `routes`: each token names 8 different experts; picks 2 j and 2 j + 1 of a token lie in one node group (expert e is in group e // 8), and the four groups of a token differ. The 16 tokens of one device name one expert at most 2 times and one node group at most 8 times.
All inputs are finite; a program needn't handle non-finite values.
Results may differ from a plain program's by a relative error of at most 0.012.
Values may be sent and summed in bfloat16 or wider, within the bound.
A program may use at most 128 MiB of HBM per device.

v0:
```python
import jax
import jax.numpy as jnp
from jax import lax
from jax.sharding import PartitionSpec as P


def expert_backward(input_rows, grad_rows, gate_proj, up_proj, down_proj):
    pre_gate = jnp.dot(input_rows, gate_proj, preferred_element_type=jnp.float32)
    pre_up = jnp.dot(input_rows, up_proj, preferred_element_type=jnp.float32)
    grad_hidden = jnp.dot(grad_rows, down_proj.T, preferred_element_type=jnp.float32)
    sigmoid = jax.nn.sigmoid(pre_gate)
    activated = pre_gate * sigmoid
    gate_score = jnp.sum(activated * pre_up * grad_hidden, axis=-1).astype(jnp.bfloat16)
    grad_gate = (grad_hidden * pre_up * sigmoid * (1.0 + pre_gate * (1.0 - sigmoid))).astype(
        jnp.bfloat16
    )
    grad_up = (grad_hidden * activated).astype(jnp.bfloat16)
    row_grad = jnp.dot(grad_gate, gate_proj.T, preferred_element_type=jnp.float32)
    row_grad = row_grad + jnp.dot(grad_up, up_proj.T, preferred_element_type=jnp.float32)
    return (row_grad.astype(jnp.bfloat16), gate_score)


def place_rows(source, anchor, target, total_slots, blank_fill):
    slot_index = jnp.full((total_slots,), -1, jnp.int32).at[target].set(anchor, mode="drop")
    filled = slot_index >= 0
    taken_rows = source[jnp.maximum(slot_index, 0)]
    return jnp.where(filled[:, None], taken_rows, blank_fill)


def rank_within(labels, label_count):
    matches = (labels[:, None] == jnp.arange(label_count, dtype=jnp.int32)[None, :]).astype(
        jnp.int32
    )
    return jnp.sum(matches * (jnp.cumsum(matches, axis=0) - 1), axis=1)


def shards(out_grad, saved_input, routes, gate_int, w_gate, w_up, w_down):
    token_count, feature_width = out_grad.shape
    top_count = routes.shape[1]
    pair_count = top_count // 2
    node_count = lax.axis_size("node")
    local_count = lax.axis_size("local")
    device_count = node_count * local_count
    slot_size = token_count // local_count
    gate_proj = w_gate[0]
    up_proj = w_up[0]
    down_proj = w_down[0]
    flat_expert = routes.reshape(-1)
    pick_rank = rank_within(flat_expert, device_count)
    both_rows = jnp.concatenate([out_grad, saved_input], axis=1)
    gate_weight = gate_int.astype(jnp.float32) * (1.0 / 65536.0)
    zero_value = jnp.zeros((), both_rows.dtype)
    target = flat_expert * slot_size + pick_rank
    anchor = jnp.arange(token_count * top_count, dtype=jnp.int32) // top_count
    outgoing = place_rows(both_rows, anchor, target, device_count * slot_size, zero_value)
    arrived = lax.all_to_all(
        outgoing.reshape(device_count, slot_size, 2 * feature_width),
        ("node", "local"),
        split_axis=0,
        concat_axis=0,
        tiled=True,
    )
    arrived = arrived.reshape(device_count * slot_size, 2 * feature_width)
    row_grad, row_score = expert_backward(
        arrived[:, feature_width:], arrived[:, :feature_width], gate_proj, up_proj, down_proj
    )
    home_rows, home_score = (
        lax.all_to_all(
            row_grad.reshape(device_count, slot_size, feature_width),
            ("node", "local"),
            split_axis=0,
            concat_axis=0,
            tiled=True,
        ),
        lax.all_to_all(
            row_score.reshape(device_count, slot_size),
            ("node", "local"),
            split_axis=0,
            concat_axis=0,
            tiled=True,
        ),
    )
    picked = home_rows.reshape(-1, feature_width)[target].astype(jnp.float32)
    weighted = picked.reshape(token_count, pair_count, 2, feature_width) * gate_weight.reshape(
        token_count, pair_count, 2, 1
    )
    group_grad = jnp.sum(weighted, axis=2).astype(jnp.bfloat16)
    gate_grad = home_score.reshape(-1)[target].reshape(token_count, top_count)
    input_grad = jnp.sum(group_grad.astype(jnp.float32), axis=1).astype(jnp.bfloat16)
    return (input_grad, gate_grad)


def solution(mesh):
    placed = (
        P(("node", "local"), None),
        P(("node", "local"), None),
        P(("node", "local"), None),
        P(("node", "local"), None),
        P(("node", "local"), None, None),
        P(("node", "local"), None, None),
        P(("node", "local"), None, None),
    )
    return jax.shard_map(
        shards,
        mesh=mesh,
        in_specs=placed,
        out_specs=(P(("node", "local"), None), P(("node", "local"), None)),
        check_vma=False,
    )
```

profile of v0, /device:TPU:1, one launch (start us, length us, event | category | flops | bytes accessed | tf_op | source)
XLA Modules:
  0.0 169.2 jit_solution(13369230832147413368)
XLA Ops:
  0.6 0.8 copy.28
  1.4 0.7 broadcast_multiply_fusion
  2.1 0.1 eq.15
  2.2 0.1 fusion.22
  2.3 0.2 reduce_window_sum.11
  2.4 0.2 select_reduce_fusion
  2.6 0.1 copy.27
  2.7 0.1 mul.61
  2.8 1.0 scatter_custom_fusion
  3.8 1.0 pad_maximum_fusion
  4.8 4.7 %gather_fusion = bf16[256,7168]{1,0:T(8,128)(2,1)} fusion(bf16[16,7168]{1,0:T(8,128)(2,1)S(1)} %pad_maximum_fusion, s32[1024]{0:T(1024)S(1)} %pad_clamp_fusion.1), kind=kCustom, calls=%fused_computation | custom fusion | bytes 7341056 | tf_op jit(solution)/shard_map/gather | solution.py:26
  9.5 8.1 %gather.12 = bf16[128,2,7168]{2,1,0:T(2,128)(2,1)} reshape(bf16[256,7168]{1,0:T(8,128)(2,1)} %gather_fusion) | data formatting | bytes 7340032 | tf_op jit(solution)/shard_map/gather | solution.py:26
  17.6 0.2 broadcast_in_dim.26
  17.7 5.2 %broadcast_select_fusion = bf16[128,2,7168]{2,1,0:T(2,128)(2,1)S(1)} fusion(bf16[128,2,7168]{2,1,0:T(2,128)(2,1)} %gather.12, pred[128,2]{1,0:T(8,128)(4,1)S(1)} %broadcast_in_dim.26), kind=kLoop, calls=%fused_computation.14 | loop fusion | flops 1835008 | bytes 7340288 | tf_op jit(solution)/shard_map/jit(_where)/select_n | solution.py:27
  22.9 58.8 %all_to_all.16 = bf16[128,2,7168]{2,1,0:T(2,128)(2,1)} all-to-all(bf16[128,2,7168]{2,1,0:T(2,128)(2,1)S(1)} %broadcast_select_fusion), channel_id=1, replica_groups=mesh['node'=16,'local'=8] {'node','local'}, dimensions={0} | all-to-all | bytes 7340032 | tf_op jit(solution)/shard_map/all_to_all | solution.py:56
  81.8 8.4 %reshape.79 = bf16[256,7168]{1,0:T(8,128)(2,1)} reshape(bf16[128,2,7168]{2,1,0:T(2,128)(2,1)} %all_to_all.16) | data formatting | bytes 7340032 | tf_op jit(solution)/shard_map/reshape | solution.py:63
  90.2 0.0 copy-start
  90.2 0.0 slice-start
  90.2 0.0 slice-start.2
  90.2 5.8 %fusion.2 = f32[256,1024]{1,0:T(8,128)S(1)} fusion(bf16[1,3584,1024]{2,1,0:T(8,128)(2,1)} %param.11, bf16[256,7168]{1,0:T(8,128)(2,1)} %reshape.79), kind=kOutput, calls=%fused_computation.6 | convolution fusion | flops 1879048192 | bytes 10223616 | tf_op jit(solution)/shard_map/dot_general | solution.py:8
  96.0 0.0 copy-done
  96.0 0.0 slice-start.1
  96.0 0.0 slice-start.3
  96.0 5.4 %fusion.6 = f32[256,1024]{1,0:T(8,128)S(1)} fusion(bf16[1,3584,1024]{2,1,0:T(8,128)(2,1)} %param.12, bf16[256,7168]{1,0:T(8,128)(2,1)S(1)} %copy-done), kind=kOutput, calls=%fused_computation.10 | convolution fusion | flops 1879048192 | bytes 10223616 | tf_op jit(solution)/shard_map/dot_general | solution.py:9
  101.5 0.0 slice-done
  101.5 0.0 slice-done.1
  101.5 2.3 %multiply_reduce_fusion.1 = (bf16[256]{0:T(256)(128)(2,1)S(1)}, f32[256,1024]{1,0:T(8,128)S(1)}) fusion(f32[256,1024]{1,0:T(8,128)S(1)} %fusion.6, f32[256,1024]{1,0:T(8,128)S(1)} %fusion.2, bf16[1,1024,3584]{2,1,0:T(8,128)(2,1)S(1)} %bitcast.28, bf16[256,7168]{1,0:T(8,128)(2,1)S(1)} %copy-done), kind=kOutput, calls=%fused_computation.21 | convolution fusion | flops 1880882944 | bytes 12321280 | tf_op jit(solution)/shard_map/dot_general | solution.py:10
  103.8 0.0 copy-start.2
  103.8 0.0 slice-done.2
  103.8 0.0 slice-done.3
  103.8 4.1 %fusion = f32[256,3584]{1,0:T(8,128)} fusion(bf16[1,3584,1024]{2,1,0:T(8,128)(2,1)S(1)} %bitcast.30, f32[256,1024]{1,0:T(8,128)S(1)} %fusion.2, f32[256,1024]{1,0:T(8,128)S(1)} %get-tuple-element.13, f32[256,1024]{1,0:T(8,128)S(1)} %fusion.6), kind=kOutput, calls=%fused_computation.4 | convolution fusion | flops 1881669632 | bytes 14155776 | tf_op jit(solution)/shard_map/dot_general | solution.py:18
  107.9 0.0 copy-done.2
  107.9 0.8 convert_element_type.52
  108.7 4.3 %all-to-all-start.2 = ((bf16[128,1,2]{2,1,0:T(2,128)(2,1)}), bf16[128,1,2]{2,1,0:T(2,128)(2,1)S(1)}, u32[]{:S(2)}, u32[]{:S(2)}) async-start(bf16[128,1,2]{2,1,0:T(2,128)(2,1)} %convert_element_type.52), calls=%async_computation.2 | async-start | bytes 131072 | tf_op jit(solution)/shard_map/all_to_all | solution.py:75
  113.0 6.6 %fusion.13 = bf16[256,3584]{1,0:T(8,128)(2,1)S(1)} fusion(f32[256,3584]{1,0:T(8,128)} %fusion, bf16[1,3584,1024]{2,1,0:T(8,128)(2,1)} %param.12, f32[256,1024]{1,0:T(8,128)} %copy-done.2, f32[256,1024]{1,0:T(8,128)S(1)} %fusion.2), kind=kOutput, calls=%fused_computation.16 | convolution fusion | flops 1882456064 | bytes 14942208 | tf_op jit(solution)/shard_map/dot_general | solution.py:19
  119.6 0.0 copy-start.1
  119.6 1.7 reshape.80
  121.2 1.4 all-to-all-done.2
  122.7 8.9 %all-to-all-start.1 = ((bf16[128,2,3584]{2,1,0:T(2,128)(2,1)}), bf16[128,2,3584]{2,1,0:T(2,128)(2,1)}, u32[]{:S(2)}, u32[]{:S(2)}) async-start(bf16[128,2,3584]{2,1,0:T(2,128)(2,1)} %reshape.80), calls=%async_computation.1 | async-start | bytes 3670016 | tf_op jit(solution)/shard_map/all_to_all | solution.py:68
  131.6 0.0 copy-done.1
  131.6 0.1 copy.29
  131.7 0.2 reduce.1
  131.9 0.1 reshape.82
  132.0 1.2 gather_fusion.2
  133.3 0.1 reshape.83
  133.4 0.7 copy.32
  134.0 25.0 %all-to-all-done.1 = bf16[128,2,3584]{2,1,0:T(2,128)(2,1)} async-done(((bf16[128,2,3584]{2,1,0:T(2,128)(2,1)}), bf16[128,2,3584]{2,1,0:T(2,128)(2,1)}, u32[]{:S(2)}, u32[]{:S(2)}) %all-to-all-start.1) | async-done | bytes 1835040 | tf_op jit(solution)/shard_map/all_to_all | solution.py:68
  159.0 4.1 %reshape.81 = bf16[256,3584]{1,0:T(8,128)(2,1)S(1)} reshape(bf16[128,2,3584]{2,1,0:T(2,128)(2,1)} %all-to-all-done.1) | data formatting | bytes 3670016 | tf_op jit(solution)/shard_map/reshape | solution.py:83
  163.1 1.1 gather_fusion.1
  164.2 1.1 reshape.84
  165.3 2.7 %multiply_reduce_fusion = bf16[16,4,3584]{2,1,0:T(4,128)(2,1)S(1)} fusion(f32[16,4,2,3584]{3,2,1,0:T(2,128)S(1)} %reshape.84, f32[16,4,2]{2,1,0:T(4,128)S(1)} %copy.29), kind=kLoop, calls=%fused_computation.18 | loop fusion | flops 688128 | bytes 2294272 | tf_op jit(solution)/shard_map/reduce_sum | solution.py:87
  168.0 1.2 convert_reduce_fusion
  (9 shorter events, 0.0 us)
Async XLA Ops:
  90.2 5.9 %copy-start = (bf16[256,7168]{1,0:T(8,128)(2,1)S(1)}, bf16[256,7168]{1,0:T(8,128)(2,1)}, u32[]{:S(2)}) copy-start(bf16[256,7168]{1,0:T(8,128)(2,1)} %reshape.79) | copy-start | bytes 11010052
  90.2 11.3 %slice-start = ((s8[7340032]{0:T(1024)(128)(4,1)}), s8[4194304]{0:T(1024)(128)(4,1)S(1)}, s32[]{:S(2)}) async-start(s8[7340032]{0:T(1024)(128)(4,1)} %bitcast.27), calls=%async_computation.3 | async-start | bytes 8388608
  90.2 13.6 %slice-start.2 = ((s8[7340032]{0:T(1024)(128)(4,1)}), s8[4194304]{0:T(1024)(128)(4,1)S(1)}, s32[]{:S(2)}) async-start(s8[7340032]{0:T(1024)(128)(4,1)} %bitcast.29), calls=%async_computation.5 | async-start | bytes 8388608
  96.0 5.5 %slice-start.1 = ((s8[7340032]{0:T(1024)(128)(4,1)}), s8[3145728]{0:T(1024)(128)(4,1)S(1)}, s32[]{:S(2)}) async-start(s8[7340032]{0:T(1024)(128)(4,1)} %bitcast.27), calls=%async_computation.4 | async-start | bytes 6291456
  96.0 7.8 %slice-start.3 = ((s8[7340032]{0:T(1024)(128)(4,1)}), s8[3145728]{0:T(1024)(128)(4,1)S(1)}, s32[]{:S(2)}) async-start(s8[7340032]{0:T(1024)(128)(4,1)} %bitcast.29), calls=%async_computation.6 | async-start | bytes 6291456
  103.8 4.2 %copy-start.2 = (f32[256,1024]{1,0:T(8,128)}, f32[256,1024]{1,0:T(8,128)S(1)}, u32[]{:S(2)}) copy-start(f32[256,1024]{1,0:T(8,128)S(1)} %get-tuple-element.13) | copy-start | bytes 3145732
  108.7 13.9 %all-to-all-start.2 = ((bf16[128,1,2]{2,1,0:T(2,128)(2,1)}), bf16[128,1,2]{2,1,0:T(2,128)(2,1)S(1)}, u32[]{:S(2)}, u32[]{:S(2)}) async-start(bf16[128,1,2]{2,1,0:T(2,128)(2,1)} %convert_element_type.52), calls=%async_computation.2 | async-start | bytes 131072 | tf_op jit(solution)/shard_map/all_to_all | solution.py:75
  119.6 12.0 %copy-start.1 = (s32[16,8]{0,1:T(8,128)S(1)}, s32[16,8]{0,1:T(8,128)}, u32[]{:S(2)}) copy-start(s32[16,8]{0,1:T(8,128)} %param.10) | copy-start | bytes 1540
  122.7 36.4 %all-to-all-start.1 = ((bf16[128,2,3584]{2,1,0:T(2,128)(2,1)}), bf16[128,2,3584]{2,1,0:T(2,128)(2,1)}, u32[]{:S(2)}, u32[]{:S(2)}) async-start(bf16[128,2,3584]{2,1,0:T(2,128)(2,1)} %reshape.80), calls=%async_computation.1 | async-start | bytes 3670016 | tf_op jit(solution)/shard_map/all_to_all | solution.py:68
where the time goes:
time: 170 us; the launch traced here: 169 us
  blocking collectives  58.8 us (35%)
  local copies, waits for them, and re-layouts  34.4 us (20%)
  waiting for transfers between devices  26.4 us (16%)
  matrix products  24.2 us (14%)
  starting transfers between devices  13.1 us (8%)
  other arithmetic  11.4 us (7%)
    all_to_all x1, blocking collectives, shards(): lax.all_to_all(outgoing.reshape(device_count, slot_size, 2 * feature_widt...  58.8 us
    all_to_all x1, waiting for transfers between devices, shards(): lax.all_to_all(row_grad.reshape(device_count, slot_size, feature_width),...  25 us
    gather x2, local copies, waits for them, and re-layouts, place_rows(): taken_rows = source[jnp.maximum(slot_index, 0)]  12.8 us
    all_to_all x1, starting transfers between devices, shards(): lax.all_to_all(row_grad.reshape(device_count, slot_size, feature_width),...  8.89 us
    reshape x1, local copies, waits for them, and re-layouts, shards(): arrived = arrived.reshape(device_count * slot_size, 2 * feature_width)  8.4 us
    dot_general x1, matrix products, expert_backward(): jnp.dot(grad_up, up_proj.T, preferred_element_type=jnp.float32)  6.56 us
    dot_general x1, matrix products, expert_backward(): jnp.dot(input_rows, gate_proj, preferred_element_type=jnp.float32)  5.84 us
    dot_general x1, matrix products, expert_backward(): pre_up = jnp.dot(input_rows, up_proj, preferred_element_type=jnp.float32)  5.41 us
  transfers between devices with their start and end apart: 2, of which 2 were waited for; matrix products, arithmetic and copies ran while one was open for 6% of the time, Pallas kernels for 0%

commit v1 on v0

v1 whole, which is shorter than its diff:
```python
import functools

import jax
import jax.numpy as jnp
from jax import lax
from jax.experimental import pallas as pl
from jax.experimental.pallas import tpu as pltpu
from jax.sharding import PartitionSpec as P

MESH = pl.DeviceIdType.MESH
BF = jnp.bfloat16
F32 = jnp.float32

ORDERS = (("x", "y", "z"), ("y", "z", "x"), ("z", "x", "y"))
WIDTHS = (1152, 1152, 1280)
OFFS = (0, 1152, 2304)
BACK_W = (512, 640, 640)
BACK_OFF = (0, 512, 1152)
BW = 640
STRIDE = {"z": 32, "y": 8, "x": 2}
SPLIT = {"z": 64, "y": 16, "x": 4}
NT = (((1,), (1,)), ((), ()))
TN = (((0,), (0,)), ((), ()))


def coords():
    node = lax.axis_index("node")
    local = lax.axis_index("local")
    return {"z": node // 4, "y": node % 4, "x": local // 2}, local % 2


def native_row(row, order):
    value = {a: (row // SPLIT[a]) % 4 for a in "xyz"}
    a1, a2, a3 = order
    return value[a3] * 64 + value[a2] * 16 + value[a1] * 4 + row % 4


def dot(a, b):
    return jnp.dot(a, b, preferred_element_type=F32)


def kernel(
    og, si, routes, gate_int, wg_hbm, wu_hbm, wd_hbm, out, gout,
    b0, b1, b2, mown, mrecv, ms, smat, kmask, sb0, sb1, sb2, gb, gr, xx, r1, r2,
    wg, wu, wd, gg, gu, score, ys, yr, zs, zr, vs, vr, fin, outs,
    wsem, s0, e0, sm1, em1, s1, e1, sm2, em2, s2, e2, s3, e3, sg, eg, t3, f3, t2, f2, t1, f1, t0, f0,
):
    pos, core = coords()
    bb, sb = (b0, b1, b2), (sb0, sb1, sb2)

    def at(axis, d, cc):
        p = dict(pos)
        p[axis] = (pos[axis] + d) % 4
        return (p["z"] * 4 + p["y"], p["x"] * 2 + (core + cc) % 2)

    def remote(src, dst, send, recv, axis, d, cc):
        return pltpu.make_async_remote_copy(
            src_ref=src, dst_ref=dst, send_sem=send, recv_sem=recv, device_id=at(axis, d, cc), device_id_type=MESH
        )

    loads = [
        pltpu.make_async_copy(hbm.at[0], vmem, wsem.at[i])
        for i, (hbm, vmem) in enumerate(((wg_hbm, wg), (wu_hbm, wu), (wd_hbm, wd)))
    ]
    for copy in loads:
        copy.start()

    barrier = pltpu.get_barrier_semaphore()
    partners = [("x", 0, 1)] + [(a, d, cc) for a in "xyz" for d in (1, 2, 3) for cc in (0, 1)]
    for a, d, cc in partners:
        pl.semaphore_signal(barrier, inc=1, device_id=at(a, d, cc), device_id_type=MESH)

    gate_i = gate_int[...]
    table = jnp.concatenate([routes[...], gate_i // 256, gate_i % 256], axis=1).astype(F32).astype(BF)
    token = lax.broadcasted_iota(jnp.int32, (16, 128), 0)
    lane = lax.broadcasted_iota(jnp.int32, (16, 128), 1)
    for q, (a1, a2, a3) in enumerate(ORDERS):
        place = (lane == pos[a1] * 32 + core * 16 + token).astype(F32).astype(BF)
        laid = lax.dot_general(table, place, TN, preferred_element_type=F32)
        mown[q, 0:8, :] = laid[0:8]
        mown[q, 8:16, :] = laid[8:16] * 256.0 + laid[16:24]

    pl.semaphore_wait(barrier, len(partners))

    def split(q, mine, other):
        a1, a2, a3 = ORDERS[q]
        rows = pl.ds(pl.multiple_of(pos[a1] * 32 + core * 16, 16), 16)
        cols = pl.ds(OFFS[q], WIDTHS[q])
        dst = bb[q].at[pos[a2], rows, :]
        return (
            pltpu.make_async_copy(mine.at[:, cols], dst, s0.at[q, 0]),
            remote(other.at[:, cols], dst, s0.at[q, 1], e0.at[q], "x", 0, 1),
        )

    for which, (mine, other) in enumerate(((og, si), (si, og))):

        @pl.when(core == which)
        def _(mine=mine, other=other):
            for q in range(3):
                for copy in split(q, mine, other):
                    copy.start()

    hops = [(d, cc) for d in range(4) for cc in range(2) if (d, cc) != (0, 0)]
    metas = {}
    for q, (a1, a2, a3) in enumerate(ORDERS):
        for d, cc in hops:
            copy = remote(
                mown.at[q], mrecv.at[q, pos[a1] * 2 + core], sm1.at[q, d, cc], em1.at[q, d, cc], a1, d, cc
            )
            copy.start()
            metas[q, d, cc] = copy
        mrecv[q, pos[a1] * 2 + core] = mown[q]

    firsts = {}
    for q, (a1, a2, a3) in enumerate(ORDERS):
        for copy in split(q, og, si):
            copy.wait()
        mine = bb[q].at[pos[a2], pl.ds(pl.multiple_of(pos[a1] * 32, 32), 32), :]
        for d in (2, 1, 3):
            firsts[q, d] = remote(mine, mine, s1.at[q, d], e1.at[q, d], a1, d, 0)
            firsts[q, d].start()

    meta2 = {}
    for q, (a1, a2, a3) in enumerate(ORDERS):
        for d, cc in hops:
            metas[q, d, cc].wait()
        ms[q, pos[a2]] = jnp.sum(mrecv[q], axis=0)
        for d in (1, 2, 3):
            meta2[q, d] = remote(ms.at[q, pos[a2]], ms.at[q, pos[a2]], sm2.at[q, d], em2.at[q, d], a2, d, 0)
            meta2[q, d].start()

    seconds = {}
    for q, (a1, a2, a3) in enumerate(ORDERS):
        for d in (1, 2, 3):
            firsts[q, d].wait()
        for d in (2, 1, 3):
            seconds[q, d] = remote(bb[q].at[pos[a2]], bb[q].at[pos[a2]], s2.at[q, d], e2.at[q, d], a2, d, 0)
            seconds[q, d].start()

    up = lax.broadcasted_iota(jnp.int32, (128, 128), 0)
    across = lax.broadcasted_iota(jnp.int32, (128, 128), 1)
    earlier = ((up < across) & (up // 16 == across // 16)).astype(F32).astype(BF)
    lanes3 = lax.broadcasted_iota(jnp.int32, (8, 16, 128), 2)
    slots3 = lax.broadcasted_iota(jnp.int32, (8, 16, 128), 1).astype(F32)
    picks3 = lax.broadcasted_iota(jnp.int32, (8, 8, 128), 1).astype(F32)
    expert3 = lax.broadcasted_iota(jnp.int32, (8, 8, 128), 0)
    pair = ((lax.broadcasted_iota(jnp.int32, (8, 128), 1) // 16) * 2).astype(F32)

    def tables(q, block):
        a1, a2, a3 = ORDERS[q]
        base = pos[a1] * STRIDE[a1] + pos[a2] * STRIDE[a2]
        expert = ((expert3 // 2) * STRIDE[a3] + expert3 % 2 + base).astype(F32)
        meta = ms[q, block]
        hit = jnp.where(meta[0:8][None] == expert, 1.0, 0.0)
        named = jnp.sum(hit, axis=1)
        rank = dot(named.astype(BF), earlier)
        code = jnp.where(named > 0.5, pair + rank, -1.0)
        chosen = jnp.where(code[:, None, :] == slots3, 1.0, 0.0)
        smat[q, block] = chosen.reshape(128, 128).astype(BF)
        if q == 0:
            rows = pl.ds(pl.multiple_of(block * 16, 16), 16)
            gate = jnp.sum(hit * meta[8:16][None], axis=1)
            gate = jnp.sum(chosen * gate[:, None, :], axis=2, keepdims=True)
            gb[:, rows, :] = jnp.broadcast_to(gate * (1.0 / 65536.0), (8, 16, 128))
            pick = jnp.sum(hit * picks3, axis=1)
            pick = jnp.sum(chosen * pick[:, None, :], axis=2, keepdims=True)
            kmask[block] = jnp.where(lanes3.astype(F32) == pick, 1.0, 0.0).reshape(128, 128).astype(BF)

    def pack(q, block):
        rows = pl.ds(pl.multiple_of(block * 16, 16), 16)
        taken = dot(smat[q, block], bb[q][block])
        sb[q][:, rows, :] = taken.astype(BF).reshape(8, 16, WIDTHS[q])

    for q, (a1, a2, a3) in enumerate(ORDERS):
        for d in (1, 2, 3):
            meta2[q, d].wait()

        def each(block, carry, q=q):
            tables(q, block)
            return carry

        lax.fori_loop(0, 4, each, 0)

    gates = {}
    gmine = gr.at[pl.ds(pl.multiple_of(pos["z"] * 64, 64), 64), :]
    for d in range(4):
        src = gb.at[((pos["z"] + d) % 4) * 2 + core]
        gates[d] = pltpu.make_async_copy(src, gmine, sg.at[d]) if d == 0 else remote(
            src, gmine, sg.at[d], eg.at[d], "z", d, 0
        )
        gates[d].start()

    thirds = {}
    for q, (a1, a2, a3) in enumerate(ORDERS):
        pack(q, pos[a2])
        for d in (1, 3, 2):
            seconds[q, d].wait()
        for d in (1, 2, 3):
            pack(q, (pos[a2] + d) % 4)
        rows = pl.ds(pl.multiple_of(pos[a3] * 64, 64), 64)
        land = xx.at[core, rows, pl.ds(0, WIDTHS[0])] if q == 0 else (r1, r2)[q - 1].at[core, rows, :]
        for d in (2, 1, 3, 0):
            for cc in (1, 0):
                src = sb[q].at[((pos[a3] + d) % 4) * 2 + (core + cc) % 2]
                if (d, cc) == (0, 0):
                    copy = pltpu.make_async_copy(src, land, s3.at[q, 0, 0])
                else:
                    copy = remote(src, land, s3.at[q, d, cc], e3.at[q, d, cc], a3, d, cc)
                copy.start()
                thirds[q, d, cc] = copy

    iota_r = lax.broadcasted_iota(jnp.int32, (256, 256), 0)
    iota_c = lax.broadcasted_iota(jnp.int32, (256, 256), 1)
    for q in range(3):
        for d in range(4):
            for cc in (0, 1):
                thirds[q, d, cc].wait()
        if q:
            perm = (native_row(iota_r, ORDERS[q]) == iota_c).astype(F32).astype(BF)
            for kind in range(2):
                xx[kind, :, OFFS[q] : OFFS[q] + WIDTHS[q]] = dot(perm, (r1, r2)[q - 1][kind]).astype(BF)
    for d in range(4):
        gates[d].wait()
    for copy in loads:
        copy.wait()

    score[...] = jnp.zeros_like(score)

    def hidden(n, carry):
        at_n = pl.ds(pl.multiple_of(n * 256, 256), 256)
        pre_gate = dot(xx[1], wg[:, at_n])
        pre_up = dot(xx[1], wu[:, at_n])
        grad_hidden = lax.dot_general(xx[0], wd[at_n, :], NT, preferred_element_type=F32)
        sig = jax.nn.sigmoid(pre_gate)
        act = pre_gate * sig
        grad_up = grad_hidden * act
        part = grad_up * pre_up
        score[...] += part[:, 0:128] + part[:, 128:256]
        gu[:, at_n] = grad_up.astype(BF)
        gg[:, at_n] = (grad_hidden * pre_up * sig * (1.0 + pre_gate * (1.0 - sig))).astype(BF)
        return carry

    lax.fori_loop(0, 4, hidden, 0)

    backs = {}
    for q, (a1, a2, a3) in enumerate(ORDERS):
        w = BACK_W[q]
        for half in range(2):
            cols = pl.ds(half * 1792 + BACK_OFF[q], w)
            rows = lax.dot_general(gg[...], wg[cols, :], NT, preferred_element_type=F32)
            rows = rows + lax.dot_general(gu[...], wu[cols, :], NT, preferred_element_type=F32)
            rows = (rows * gr[:, 0:1]).astype(BF)
            if q:
                back = (native_row(iota_c, ORDERS[q]) == iota_r).astype(F32).astype(BF)
                rows = dot(back, rows).astype(BF)
            else:
                total = jnp.sum(score[...], axis=1, keepdims=True)
                ys[q, half, :, w:BW] = jnp.broadcast_to(total, (256, 128)).astype(BF)
            ys[q, half, :, 0:w] = rows
        mine = yr.at[q, pos[a3] * 2 + core]
        for d in (2, 1, 3, 0):
            for cc in (1, 0):
                there = pl.ds(pl.multiple_of(((pos[a3] + d) % 4) * 64, 64), 64)
                src = ys.at[q, (core + cc) % 2, there, :]
                if (d, cc) == (0, 0):
                    copy = pltpu.make_async_copy(src, mine, t3.at[q, 0, 0])
                else:
                    copy = remote(src, mine, t3.at[q, d, cc], f3.at[q, d, cc], a3, d, cc)
                copy.start()
                backs[q, d, cc] = copy

    sums = {}
    for q, (a1, a2, a3) in enumerate(ORDERS):
        for d in range(4):
            for cc in (0, 1):
                backs[q, d, cc].wait()
        for d in (2, 1, 3, 0):
            block = (pos[a2] + d) % 4
            rows = pl.ds(pl.multiple_of(block * 16, 16), 16)
            got = yr[q, :, rows, :].reshape(128, BW)
            if q == 0:
                got = jnp.concatenate([got[:, 0:512], got[:, 512:640] * kmask[block]], axis=1)
            total = lax.dot_general(smat[q, block], got, TN, preferred_element_type=F32).astype(BF)
            if d == 0:
                zr[q, pos[a2]] = total
            else:
                zs[q, block] = total
                sums[q, d] = remote(zs.at[q, block], zr.at[q, pos[a2]], t2.at[q, d], f2.at[q, d], a2, d, 0)
                sums[q, d].start()

    lasts = {}
    for q, (a1, a2, a3) in enumerate(ORDERS):
        for d in (1, 3, 2):
            sums[q, d].wait()
        total = jnp.zeros((128, BW), F32)
        for s in range(4):
            total = total + zr[q, s].astype(F32)
        vs[q] = total.astype(BF)
        for d in (2, 1, 3):
            there = pl.ds(pl.multiple_of(((pos[a1] + d) % 4) * 32, 32), 32)
            lasts[q, d] = remote(vs.at[q, there, :], vr.at[q, pos[a1]], t1.at[q, d], f1.at[q, d], a1, d, 0)
            lasts[q, d].start()
        vr[q, pos[a1]] = vs[q, pl.ds(pl.multiple_of(pos[a1] * 32, 32), 32), :]

    for q, (a1, a2, a3) in enumerate(ORDERS):
        for d in (1, 3, 2):
            lasts[q, d].wait()
        total = jnp.zeros((32, BW), F32)
        for s in range(4):
            total = total + vr[q, s].astype(F32)
        fin[:, q * BW : (q + 1) * BW] = total.astype(BF)

    own = pl.ds(pl.multiple_of(core * 16, 16), 16)
    sibling = pl.ds(pl.multiple_of((1 - core) * 16, 16), 16)
    copy = remote(fin.at[sibling, :], outs.at[core], t0.at[0], f0.at[0], "x", 0, 1)
    copy.start()
    outs[core] = fin[own, :]
    gout[...] = fin[own, 512:520]
    copy.wait()
    for half in range(2):
        for q in range(3):
            start = half * 1792 + BACK_OFF[q]
            out[:, start : start + BACK_W[q]] = outs[half, :, q * BW : q * BW + BACK_W[q]]


def shards(out_grad, saved_input, routes, gate_int, w_gate, w_up, w_down):
    vmem = pl.BlockSpec(memory_space=pltpu.VMEM)
    hbm = pl.BlockSpec(memory_space=pl.ANY)
    sem = pltpu.SemaphoreType.DMA
    scratch = (
        [pltpu.VMEM((4, 128, w), BF) for w in WIDTHS]
        + [
            pltpu.VMEM((3, 16, 128), F32),
            pltpu.VMEM((3, 8, 16, 128), F32),
            pltpu.VMEM((3, 4, 16, 128), F32),
            pltpu.VMEM((3, 4, 128, 128), BF),
            pltpu.VMEM((4, 128, 128), BF),
        ]
        + [pltpu.VMEM((8, 64, w), BF) for w in WIDTHS]
        + [
            pltpu.VMEM((8, 64, 128), F32),
            pltpu.VMEM((256, 128), F32),
            pltpu.VMEM((2, 256, 3584), BF),
            pltpu.VMEM((2, 256, WIDTHS[1]), BF),
            pltpu.VMEM((2, 256, WIDTHS[2]), BF),
            pltpu.VMEM((3584, 1024), BF),
            pltpu.VMEM((3584, 1024), BF),
            pltpu.VMEM((1024, 3584), BF),
            pltpu.VMEM((256, 1024), BF),
            pltpu.VMEM((256, 1024), BF),
            pltpu.VMEM((256, 128), F32),
            pltpu.VMEM((3, 2, 256, BW), BF),
            pltpu.VMEM((3, 8, 64, BW), BF),
            pltpu.VMEM((3, 4, 128, BW), BF),
            pltpu.VMEM((3, 4, 128, BW), BF),
            pltpu.VMEM((3, 128, BW), BF),
            pltpu.VMEM((3, 4, 32, BW), BF),
            pltpu.VMEM((32, 3 * BW), BF),
            pltpu.VMEM((2, 16, 3 * BW), BF),
        ]
        + [
            sem((3,)),
            sem((3, 2)), sem((3,)),
            sem((3, 4, 2)), sem((3, 4, 2)),
            sem((3, 4)), sem((3, 4)),
            sem((3, 4)), sem((3, 4)),
            sem((3, 4)), sem((3, 4)),
            sem((3, 4, 2)), sem((3, 4, 2)),
            sem((4,)), sem((4,)),
            sem((3, 4, 2)), sem((3, 4, 2)),
            sem((3, 4)), sem((3, 4)),
            sem((3, 4)), sem((3, 4)),
            sem((1,)), sem((1,)),
        ]
    )
    return tuple(
        pl.pallas_call(
            kernel,
            out_shape=(
                jax.ShapeDtypeStruct(out_grad.shape, BF),
                jax.ShapeDtypeStruct(routes.shape, BF),
            ),
            in_specs=[hbm, hbm, vmem, vmem, hbm, hbm, hbm],
            out_specs=(vmem, vmem),
            scratch_shapes=scratch,
            compiler_params=pltpu.CompilerParams(
                collective_id=0, has_side_effects=True, vmem_limit_bytes=64 * 2**20 - 65536
            ),
        )(out_grad, saved_input, routes, gate_int, w_gate, w_up, w_down)
    )


def solution(mesh):
    rows = P(("node", "local"), None)
    experts = P(("node", "local"), None, None)
    return jax.shard_map(
        shards,
        mesh=mesh,
        in_specs=(rows, rows, rows, rows, experts, experts, experts),
        out_specs=(rows, rows),
        check_vma=False,
    )
```

time: 170 us -> 100 us (0.59)
  Pallas kernels: 0 us -> 93.6 us
  blocking collectives: 58.8 us -> 0 us
  local copies, waits for them, and re-layouts: 34.4 us -> 5.59 us
  waiting for transfers between devices: 26.4 us -> 0 us
  matrix products: 24.2 us -> 0 us
  starting transfers between devices: 13.1 us -> 0 us
  other arithmetic: 11.4 us -> 0 us
    pallas_call x0 -> x1, Pallas kernels: none -> 93.6 us  [shards(): pl.pallas_call(kernel, out_shape=(jax.ShapeDtypeStruct(out_grad.shape, BF...]
    all_to_all x1 -> x0, blocking collectives: 58.8 us -> none  [shards(): lax.all_to_all(outgoing.reshape(device_count, slot_size, 2 * feature_widt...]
    all_to_all x2 -> x0, waiting for transfers between devices: 26.4 us -> none  [the longest x1 25 us: shards(): lax.all_to_all(row_grad.reshape(device_count, slot_size, feature_width),...]
    dot_general x5 -> x0, matrix products: 24.2 us -> none  [the longest x1 6.56 us: expert_backward(): jnp.dot(grad_up, up_proj.T, preferred_element_type=jnp.float32)]
    gather x4 -> x0, local copies, waits for them, and re-layouts: 15.1 us -> none  [the longest x2 12.8 us: place_rows(): taken_rows = source[jnp.maximum(slot_index, 0)]]
    reshape x5 -> x0, local copies, waits for them, and re-layouts: 14.4 us -> none  [the longest x1 8.4 us: shards(): arrived = arrived.reshape(device_count * slot_size, 2 * feature_width)]
    all_to_all x2 -> x0, starting transfers between devices: 13.1 us -> none  [the longest x1 8.89 us: shards(): lax.all_to_all(row_grad.reshape(device_count, slot_size, feature_width),...]
    select_n x3 -> x0, other arithmetic: 5.18 us -> none  [the longest x1 5.17 us: place_rows(): return jnp.where(filled[:, None], taken_rows, blank_fill)]
  transfers between devices with their start and end apart: 2 -> 0, of which waited for: 2 -> 0; matrix products, arithmetic and copies ran while one was open for 6% -> 0% of each run, Pallas kernels for 0% -> 0%
where the time goes in v1:
time: 100 us; the launch traced here: 99.8 us
  Pallas kernels  93.6 us (94%)
  local copies, waits for them, and re-layouts  5.59 us (6%)
    pallas_call x1, Pallas kernels, shards(): pl.pallas_call(kernel, out_shape=(jax.ShapeDtypeStruct(out_grad.shape, BF...  93.6 us
    unnamed x3, local copies, waits for them, and re-layouts  4.26 us

profile of v1, /device:TPU:1, one launch (start us, length us, event | category | flops | bytes accessed | tf_op | source)
XLA Modules:
  0.0 99.8 jit_solution(5347001886302139450)
XLA Ops:
  0.6 1.4 %copy.9.routes = s32[16,8]{1,0:T(8,128)} copy(s32[16,8]{0,1:T(8,128)} %param.9) | data formatting | bytes 1024 | tf_op args[2]
  2.0 1.4 %copy.10.gate_int = s32[16,8]{1,0:T(8,128)} copy(s32[16,8]{0,1:T(8,128)} %param.10) | data formatting | bytes 1024 | tf_op args[3]
  3.3 93.6 %shard_map.86 = (bf16[16,3584]{1,0:T(8,128)(2,1)}, bf16[16,8]{1,0:T(8,128)(2,1)}) custom-call(bf16[16,3584]{1,0:T(8,128)(2,1)} %og.1, bf16[16,3584]{1,0:T(8,128)(2,1)} %si.1, s32[16,8]{1,0:T(8,128)} %copy.9.routes, s32[16,8]{1,0:T(8,128)} %copy.10.gate_int, bf16[1,3584,1024]{2,1,0:T(8,128)(2,1)} %wg_hbm.1, bf16[1,3584,1024]{2,1,0:T(8,128)(2,1)} %wu_hbm.1, ...), custom_call_target="tpu_custom_call" | custom-call | tf_op jit(solution)/shard_map/pallas_call | solution.py:377
  96.9 1.3 %copy.11 = bf16[16,8]{0,1:T(8,128)(2,1)} copy(bf16[16,8]{1,0:T(8,128)(2,1)} %get-tuple-element.3) | data formatting | bytes 512 | tf_op jit(solution)/shard_map/pallas_call | solution.py:377
  98.3 1.6 %copy.13 = bf16[16,3584]{1,0:T(8,128)(2,1)} copy(bf16[16,3584]{1,0:T(8,128)(2,1)} %get-tuple-element.6) | data formatting | bytes 229376

commit v2 on v1

v2 whole, which is shorter than its diff:
```python
import functools

import jax
import jax.numpy as jnp
from jax import lax
from jax.experimental import pallas as pl
from jax.experimental.pallas import tpu as pltpu
from jax.sharding import PartitionSpec as P

MESH = pl.DeviceIdType.MESH
BF = jnp.bfloat16
F32 = jnp.float32

ORDERS = (("x", "y", "z"), ("y", "z", "x"), ("z", "x", "y"))
HALF = 1792
WIDTHS = (640, 640, 512)
OFFS = (0, 640, 1280)
UNITS = ((0, 0), (0, 1), (0, 2), (1, 0), (1, 1), (1, 2))
BACK_W = {(0, 0): 256, (0, 1): 256, (0, 2): 256, (1, 0): 256, (1, 1): 384, (1, 2): 384}
BACK_OFF = {(0, 0): 0, (0, 1): 512, (0, 2): 1024, (1, 0): 1536, (1, 1): 2048, (1, 2): 2816}
BW = (256, 384)
FIN = {(0, 0): 0, (0, 1): 256, (0, 2): 512, (1, 0): 768, (1, 1): 1152, (1, 2): 1536}
FIN_W = 1920
STRIDE = {"z": 32, "y": 8, "x": 2}
SPLIT = {"z": 64, "y": 16, "x": 4}
NT = (((1,), (1,)), ((), ()))
TN = (((0,), (0,)), ((), ()))


def coords():
    node = lax.axis_index("node")
    local = lax.axis_index("local")
    return {"z": node // 4, "y": node % 4, "x": local // 2}, local % 2


def native_row(row, order):
    value = {a: (row // SPLIT[a]) % 4 for a in "xyz"}
    a1, a2, a3 = order
    return value[a3] * 64 + value[a2] * 16 + value[a1] * 4 + row % 4


def dot(a, b):
    return jnp.dot(a, b, preferred_element_type=F32)


def kernel(
    og, si, routes, gate_int, wg_hbm, wu_hbm, wd_hbm, out, gout,
    b0, b1, b2, mown, mrecv, msum, ms, smat, kmask, sb0, sb1, sb2, gb, gr, xx, r1, r2,
    wg, wu, wd, pre, gg, gu, score, ysa, ysb, yra, yrb, zsa, zsb, zra, zrb, vsa, vsb, vra, vrb, fin, outs,
    wsem, s0, e0, sm1, em1, s1, e1, sm2, em2, s2, e2, s3, e3, sg, eg, t3, f3, t2, f2, t1, f1, t0, f0,
):
    pos, core = coords()
    bb, sb = (b0, b1, b2), (sb0, sb1, sb2)
    ys, yr, zs, zr, vs, vr = (ysa, ysb), (yra, yrb), (zsa, zsb), (zra, zrb), (vsa, vsb), (vra, vrb)
    KINDS = (1, 0)

    def at(axis, d, cc):
        p = dict(pos)
        p[axis] = (pos[axis] + d) % 4
        return (p["z"] * 4 + p["y"], p["x"] * 2 + (core + cc) % 2)

    def remote(src, dst, send, recv, axis, d, cc):
        return pltpu.make_async_remote_copy(
            src_ref=src, dst_ref=dst, send_sem=send, recv_sem=recv, device_id=at(axis, d, cc), device_id_type=MESH
        )

    def block(index, size):
        return pl.ds(pl.multiple_of(index * size, size), size)

    loads = [
        pltpu.make_async_copy(hbm.at[0], vmem, wsem.at[i])
        for i, (hbm, vmem) in enumerate(((wg_hbm, wg), (wu_hbm, wu), (wd_hbm, wd)))
    ]
    for copy in loads:
        copy.start()

    barrier = pltpu.get_barrier_semaphore()
    partners = [("x", 0, 1)] + [(a, d, cc) for a in "xyz" for d in (1, 2, 3) for cc in (0, 1)]
    for a, d, cc in partners:
        pl.semaphore_signal(barrier, inc=1, device_id=at(a, d, cc), device_id_type=MESH)

    gate_i = gate_int[...]
    table = jnp.concatenate([routes[...], gate_i // 256, gate_i % 256], axis=0).astype(F32).astype(BF)
    token = lax.broadcasted_iota(jnp.int32, (16, 128), 0)
    lane = lax.broadcasted_iota(jnp.int32, (16, 128), 1)
    for q, (a1, a2, a3) in enumerate(ORDERS):
        place = (lane == pos[a1] * 32 + core * 16 + token).astype(F32).astype(BF)
        laid = dot(table, place)
        mown[q, 0:8, :] = laid[0:8]
        mown[q, 8:16, :] = laid[8:16] * 256.0 + laid[16:24]

    pl.semaphore_wait(barrier, len(partners))

    splits = {}
    for k in KINDS:
        source = (og, si)[k]
        for q, (a1, a2, a3) in enumerate(ORDERS):
            dst = bb[q].at[k, pos[a2], block(pos[a1] * 2 + core, 16), :]
            mine = pl.ds(pl.multiple_of(core * HALF + OFFS[q], 128), WIDTHS[q])
            other = pl.ds(pl.multiple_of((1 - core) * HALF + OFFS[q], 128), WIDTHS[q])
            splits[k, q, 1] = remote(source.at[:, other], dst, s0.at[k, q, 1], e0.at[k, q], "x", 0, 1)
            splits[k, q, 0] = pltpu.make_async_copy(source.at[:, mine], dst, s0.at[k, q, 0])
            splits[k, q, 1].start()
            splits[k, q, 0].start()

    hops = [(d, cc) for d in range(4) for cc in range(2) if (d, cc) != (0, 0)]
    metas = {}
    for q, (a1, a2, a3) in enumerate(ORDERS):
        for d, cc in hops:
            copy = remote(mown.at[q], mrecv.at[q, pos[a1] * 2 + core], sm1.at[q, d, cc], em1.at[q, d, cc], a1, d, cc)
            copy.start()
            metas[q, d, cc] = copy
        mrecv[q, pos[a1] * 2 + core] = mown[q]

    firsts = {}
    for k in KINDS:
        for q, (a1, a2, a3) in enumerate(ORDERS):
            splits[k, q, 0].wait()
            splits[k, q, 1].wait()
            mine = bb[q].at[k, pos[a2], block(pos[a1], 32), :]
            for d in (2, 1, 3):
                firsts[k, q, d] = remote(mine, mine, s1.at[k, q, d], e1.at[k, q, d], a1, d, 0)
                firsts[k, q, d].start()

    meta2 = {}
    for q, (a1, a2, a3) in enumerate(ORDERS):
        for d, cc in hops:
            metas[q, d, cc].wait()
        total = jnp.sum(mrecv[q], axis=0)
        msum[q] = total
        ms[q, pos[a2]] = total
        for d in (1, 2, 3):
            meta2[q, d] = remote(msum.at[q], ms.at[q, pos[a2]], sm2.at[q, d], em2.at[q, d], a2, d, 0)
            meta2[q, d].start()

    seconds = {}
    for k in KINDS:
        for q, (a1, a2, a3) in enumerate(ORDERS):
            for d in (1, 2, 3):
                firsts[k, q, d].wait()
            mine = bb[q].at[k, pos[a2]]
            for d in (1, 3):
                seconds[k, q, d] = remote(mine, mine, s2.at[k, q, d], e2.at[k, q, d], a2, d, 0)
                seconds[k, q, d].start()
    for k in KINDS:
        for q, (a1, a2, a3) in enumerate(ORDERS):
            for d, part in ((1, 0), (3, 1)):
                seconds[k, q, d].wait()
                held = bb[q].at[k, (pos[a2] - d) % 4, pl.ds(part * 64, 64), :]
                copy = remote(held, held, s2.at[k, q, d - 1], e2.at[k, q, d - 1], a2, d, 0)
                copy.start()
                seconds[k, q, d - 1] = copy

    up = lax.broadcasted_iota(jnp.int32, (256, 256), 0)
    across = lax.broadcasted_iota(jnp.int32, (256, 256), 1)
    earlier = ((up < across) & (up // 16 == across // 16)).astype(F32).astype(BF)
    lanes3 = lax.broadcasted_iota(jnp.int32, (8, 32, 128), 2).astype(F32)
    slots3 = lax.broadcasted_iota(jnp.int32, (8, 32, 256), 1).astype(F32)
    picks3 = lax.broadcasted_iota(jnp.int32, (8, 8, 256), 1).astype(F32)
    expert3 = lax.broadcasted_iota(jnp.int32, (8, 8, 256), 0)
    pair = ((lax.broadcasted_iota(jnp.int32, (8, 256), 1) // 16) * 2).astype(F32)

    def tables(q, p):
        a1, a2, a3 = ORDERS[q]
        base = pos[a1] * STRIDE[a1] + pos[a2] * STRIDE[a2]
        expert = ((expert3 // 2) * STRIDE[a3] + expert3 % 2 + base).astype(F32)
        meta = jnp.concatenate([ms[q, 2 * p], ms[q, 2 * p + 1]], axis=1)
        hit = jnp.where(meta[0:8][None] == expert, 1.0, 0.0)
        named = jnp.sum(hit, axis=1)
        rank = dot(named.astype(BF), earlier)
        code = jnp.where(named > 0.5, pair + rank, -1.0)
        chosen = jnp.where(code[:, None, :] == slots3, 1.0, 0.0)
        smat[q, p] = chosen.reshape(256, 256).astype(BF)
        if q == 0:
            gate = jnp.sum(hit * meta[8:16][None], axis=1)
            gate = jnp.sum(chosen * gate[:, None, :], axis=2, keepdims=True)
            gb[:, p * 32 : p * 32 + 32, :] = jnp.broadcast_to(gate * (1.0 / 65536.0), (8, 32, 128))
            pick = jnp.sum(hit * picks3, axis=1)
            pick = jnp.sum(chosen * pick[:, None, :], axis=2, keepdims=True)
            kmask[p] = jnp.where(lanes3 == pick, 1.0, 0.0).reshape(256, 128).astype(BF)

    gates = {}
    for q, (a1, a2, a3) in enumerate(ORDERS):
        for d in (1, 2, 3):
            meta2[q, d].wait()
        for p in range(2):
            tables(q, p)
        if q == 0:
            gmine = gr.at[block(pos["z"], 64), :]
            for d in range(4):
                src = gb.at[((pos["z"] + d) % 4) * 2 + core]
                if d == 0:
                    gates[d] = pltpu.make_async_copy(src, gmine, sg.at[d])
                else:
                    gates[d] = remote(src, gmine, sg.at[d], eg.at[d], "z", d, 0)
                gates[d].start()

    thirds = {}
    for k in KINDS:
        for q, (a1, a2, a3) in enumerate(ORDERS):
            for d in (0, 2):
                seconds[k, q, d].wait()
            for p in range(2):
                rows = dot(smat[q, p], bb[q][k, 2 * p : 2 * p + 2].reshape(256, WIDTHS[q]))
                sb[q][k, :, p * 32 : p * 32 + 32, :] = rows.astype(BF).reshape(8, 32, WIDTHS[q])
            there = block(pos[a3], 64)
            if q == 0:
                land = xx.at[k, there, pl.ds(pl.multiple_of(core * HALF, 128), WIDTHS[0])]
            else:
                land = (r1, r2)[q - 1].at[k, core, there, :]
            for d in (2, 1, 3, 0):
                for cc in (1, 0):
                    src = sb[q].at[k, ((pos[a3] + d) % 4) * 2 + (core + cc) % 2]
                    if (d, cc) == (0, 0):
                        copy = pltpu.make_async_copy(src, land, s3.at[k, q, 0, 0])
                    else:
                        copy = remote(src, land, s3.at[k, q, d, cc], e3.at[k, q, d, cc], a3, d, cc)
                    copy.start()
                    thirds[k, q, d, cc] = copy

    iota_r = lax.broadcasted_iota(jnp.int32, (256, 256), 0)
    iota_c = lax.broadcasted_iota(jnp.int32, (256, 256), 1)

    def arrive(k):
        for q in range(3):
            for d in range(4):
                for cc in (0, 1):
                    thirds[k, q, d, cc].wait()
            if q:
                perm = (native_row(iota_r, ORDERS[q]) == iota_c).astype(F32).astype(BF)
                for half in range(2):
                    start = half * HALF + OFFS[q]
                    rows = dot(perm, (r1, r2)[q - 1][k, half])
                    xx[k, :, start : start + WIDTHS[q]] = rows.astype(BF)

    arrive(1)
    for copy in loads:
        copy.wait()

    def forward(n, carry):
        at_n = block(n, 512)
        pre[0, :, at_n] = dot(xx[1], wg[:, at_n])
        pre[1, :, at_n] = dot(xx[1], wu[:, at_n])
        return carry

    lax.fori_loop(0, 2, forward, 0)
    arrive(0)
    score[...] = jnp.zeros_like(score)

    def backward(n, carry):
        at_n = block(n, 512)
        grad_hidden = lax.dot_general(xx[0], wd[at_n, :], NT, preferred_element_type=F32)
        pre_gate = pre[0, :, at_n]
        pre_up = pre[1, :, at_n]
        sig = jax.nn.sigmoid(pre_gate)
        act = pre_gate * sig
        grad_up = grad_hidden * act
        part = grad_up * pre_up
        score[...] += (part[:, 0:128] + part[:, 128:256]) + (part[:, 256:384] + part[:, 384:512])
        gu[:, at_n] = grad_up.astype(BF)
        gg[:, at_n] = (grad_hidden * pre_up * sig * (1.0 + pre_gate * (1.0 - sig))).astype(BF)
        return carry

    lax.fori_loop(0, 2, backward, 0)
    for d in range(4):
        gates[d].wait()

    backs = {}

    def expert_rows(t, q):
        a1, a2, a3 = ORDERS[q]
        w = BACK_W[t, q]
        cols = pl.ds(BACK_OFF[t, q], 2 * w)
        rows = lax.dot_general(gg[...], wg[cols, :], NT, preferred_element_type=F32)
        rows = rows + lax.dot_general(gu[...], wu[cols, :], NT, preferred_element_type=F32)
        rows = (rows * gr[:, 0:1]).astype(BF)
        if q:
            back = (native_row(iota_c, ORDERS[q]) == iota_r).astype(F32).astype(BF)
            rows = dot(back, rows).astype(BF)
        for half in range(2):
            ys[t][q, half, :, 0:w] = rows[:, half * w : (half + 1) * w]
            if w < BW[t]:
                total = jnp.sum(score[...], axis=1, keepdims=True)
                ys[t][q, half, :, w : BW[t]] = jnp.broadcast_to(total, (256, 128)).astype(BF)
        mine = yr[t].at[q, pos[a3] * 2 + core]
        for d in (2, 1, 3, 0):
            for cc in (1, 0):
                src = ys[t].at[q, (core + cc) % 2, block((pos[a3] + d) % 4, 64), :]
                if (d, cc) == (0, 0):
                    copy = pltpu.make_async_copy(src, mine, t3.at[t, q, 0, 0])
                else:
                    copy = remote(src, mine, t3.at[t, q, d, cc], f3.at[t, q, d, cc], a3, d, cc)
                copy.start()
                backs[t, q, d, cc] = copy

    sums = {}

    def combine(t, q):
        a1, a2, a3 = ORDERS[q]
        for d in range(4):
            for cc in (0, 1):
                backs[t, q, d, cc].wait()
        for p in range(2):
            got = yr[t][q, :, p * 32 : p * 32 + 32, :].reshape(256, BW[t])
            if BACK_W[t, q] < BW[t]:
                got = jnp.concatenate([got[:, 0:256], got[:, 256:384] * kmask[p]], axis=1)
            total = lax.dot_general(smat[q, p], got, TN, preferred_element_type=F32).astype(BF)
            zs[t][q, 2 * p : 2 * p + 2] = total.reshape(2, 128, BW[t])
        for d in (2, 1, 3, 0):
            src, dst = zs[t].at[q, (pos[a2] + d) % 4], zr[t].at[q, pos[a2]]
            if d == 0:
                copy = pltpu.make_async_copy(src, dst, t2.at[t, q, d])
            else:
                copy = remote(src, dst, t2.at[t, q, d], f2.at[t, q, d], a2, d, 0)
            copy.start()
            sums[t, q, d] = copy

    lasts = {}

    def narrow(t, q):
        a1, a2, a3 = ORDERS[q]
        for d in (0, 1, 3, 2):
            sums[t, q, d].wait()
        total = jnp.zeros((128, BW[t]), F32)
        for s in range(4):
            total = total + zr[t][q, s].astype(F32)
        vs[t][q] = total.astype(BF)
        for d in (2, 1, 3, 0):
            src, dst = vs[t].at[q, block((pos[a1] + d) % 4, 32), :], vr[t].at[q, pos[a1]]
            if d == 0:
                copy = pltpu.make_async_copy(src, dst, t1.at[t, q, d])
            else:
                copy = remote(src, dst, t1.at[t, q, d], f1.at[t, q, d], a1, d, 0)
            copy.start()
            lasts[t, q, d] = copy

    def finish(t, q):
        for d in (0, 1, 3, 2):
            lasts[t, q, d].wait()
        total = jnp.zeros((32, BW[t]), F32)
        for s in range(4):
            total = total + vr[t][q, s].astype(F32)
        fin[:, FIN[t, q] : FIN[t, q] + BW[t]] = total.astype(BF)

    for t, q in UNITS:
        expert_rows(t, q)
    for t, q in UNITS:
        combine(t, q)
    for t, q in UNITS:
        narrow(t, q)
    for t, q in UNITS:
        finish(t, q)

    copy = remote(fin.at[block(1 - core, 16), :], outs.at[core], t0.at[0], f0.at[0], "x", 0, 1)
    copy.start()
    outs[core] = fin[block(core, 16), :]
    same = (lax.broadcasted_iota(jnp.int32, (16, 16), 0) == lax.broadcasted_iota(jnp.int32, (16, 16), 1))
    scores = fin[block(core, 16), FIN[1, 0] + 256 : FIN[1, 0] + 384]
    turned = lax.dot_general(scores, same.astype(F32).astype(BF), TN, preferred_element_type=F32)
    gout[...] = turned[0:8].astype(BF)
    copy.wait()
    for half in range(2):
        for unit in UNITS:
            w = BACK_W[unit]
            start = BACK_OFF[unit] + half * w
            out[:, start : start + w] = outs[half, :, FIN[unit] : FIN[unit] + w]


def shards(out_grad, saved_input, routes, gate_int, w_gate, w_up, w_down):
    vmem = pl.BlockSpec(memory_space=pltpu.VMEM)
    hbm = pl.BlockSpec(memory_space=pl.ANY)
    sem = pltpu.SemaphoreType.DMA
    scratch = (
        [pltpu.VMEM((2, 4, 128, w), BF) for w in WIDTHS]
        + [
            pltpu.VMEM((3, 16, 128), F32),
            pltpu.VMEM((3, 8, 16, 128), F32),
            pltpu.VMEM((3, 16, 128), F32),
            pltpu.VMEM((3, 4, 16, 128), F32),
            pltpu.VMEM((3, 2, 256, 256), BF),
            pltpu.VMEM((2, 256, 128), BF),
        ]
        + [pltpu.VMEM((2, 8, 64, w), BF) for w in WIDTHS]
        + [
            pltpu.VMEM((8, 64, 128), F32),
            pltpu.VMEM((256, 128), F32),
            pltpu.VMEM((2, 256, 3584), BF),
            pltpu.VMEM((2, 2, 256, WIDTHS[1]), BF),
            pltpu.VMEM((2, 2, 256, WIDTHS[2]), BF),
            pltpu.VMEM((3584, 1024), BF),
            pltpu.VMEM((3584, 1024), BF),
            pltpu.VMEM((1024, 3584), BF),
            pltpu.VMEM((2, 256, 1024), F32),
            pltpu.VMEM((256, 1024), BF),
            pltpu.VMEM((256, 1024), BF),
            pltpu.VMEM((256, 128), F32),
        ]
        + [pltpu.VMEM((3, 2, 256, w), BF) for w in BW]
        + [pltpu.VMEM((3, 8, 64, w), BF) for w in BW]
        + [pltpu.VMEM((3, 4, 128, w), BF) for w in BW]
        + [pltpu.VMEM((3, 4, 128, w), BF) for w in BW]
        + [pltpu.VMEM((3, 128, w), BF) for w in BW]
        + [pltpu.VMEM((3, 4, 32, w), BF) for w in BW]
        + [
            pltpu.VMEM((32, FIN_W), BF),
            pltpu.VMEM((2, 16, FIN_W), BF),
        ]
        + [
            sem((3,)),
            sem((2, 3, 2)), sem((2, 3)),
            sem((3, 4, 2)), sem((3, 4, 2)),
            sem((2, 3, 4)), sem((2, 3, 4)),
            sem((3, 4)), sem((3, 4)),
            sem((2, 3, 4)), sem((2, 3, 4)),
            sem((2, 3, 4, 2)), sem((2, 3, 4, 2)),
            sem((4,)), sem((4,)),
            sem((2, 3, 4, 2)), sem((2, 3, 4, 2)),
            sem((2, 3, 4)), sem((2, 3, 4)),
            sem((2, 3, 4)), sem((2, 3, 4)),
            sem((1,)), sem((1,)),
        ]
    )
    input_grad, gate_grad = pl.pallas_call(
        kernel,
        out_shape=(
            jax.ShapeDtypeStruct(out_grad.shape, BF),
            jax.ShapeDtypeStruct(routes.shape[::-1], BF),
        ),
        in_specs=[hbm, hbm, vmem, vmem, hbm, hbm, hbm],
        out_specs=(vmem, vmem),
        scratch_shapes=scratch,
        compiler_params=pltpu.CompilerParams(
            collective_id=0, has_side_effects=True, vmem_limit_bytes=64 * 2**20 - 65536
        ),
    )(out_grad, saved_input, routes.T, gate_int.T, w_gate, w_up, w_down)
    return input_grad, gate_grad.T


def solution(mesh):
    rows = P(("node", "local"), None)
    experts = P(("node", "local"), None, None)
    return jax.shard_map(
        shards,
        mesh=mesh,
        in_specs=(rows, rows, rows, rows, experts, experts, experts),
        out_specs=(rows, rows),
        check_vma=False,
    )
```

time: 100 us -> 84.9 us (0.85)
  Pallas kernels: 93.6 us -> 81.3 us
  local copies, waits for them, and re-layouts: 5.59 us -> 2.8 us
    pallas_call x1, Pallas kernels: 93.6 us -> 81.3 us  [shards(): pl.pallas_call(kernel, out_shape=(jax.ShapeDtypeStruct(out_grad.shape, BF...]
    unnamed x3 -> x2, local copies, waits for them, and re-layouts: 4.26 us -> 2.8 us
    pallas_call x1 -> x0, local copies, waits for them, and re-layouts: 1.33 us -> none  [shards(): pl.pallas_call(kernel, out_shape=(jax.ShapeDtypeStruct(out_grad.shape, BF...]
where the time goes in v2:
time: 84.9 us; the launch traced here: 84.7 us
  Pallas kernels  81.3 us (96%)
  local copies, waits for them, and re-layouts  2.8 us (3%)
    pallas_call x1, Pallas kernels, shards(): pl.pallas_call(kernel, out_shape=(jax.ShapeDtypeStruct(out_grad.shape, BF...  81.3 us
    unnamed x2, local copies, waits for them, and re-layouts  2.8 us

profile of v2, /device:TPU:1, one launch (start us, length us, event | category | flops | bytes accessed | tf_op | source)
XLA Modules:
  0.0 84.7 jit_solution(2310643065839730129)
XLA Ops:
  0.6 81.3 %shard_map.86 = (bf16[16,3584]{1,0:T(8,128)(2,1)}, bf16[8,16]{1,0:T(8,128)(2,1)}) custom-call(bf16[16,3584]{1,0:T(8,128)(2,1)} %og.1, bf16[16,3584]{1,0:T(8,128)(2,1)} %si.1, s32[8,16]{1,0:T(8,128)} %bitcast.3, s32[8,16]{1,0:T(8,128)} %bitcast.4, bf16[1,3584,1024]{2,1,0:T(8,128)(2,1)} %wg_hbm.1, bf16[1,3584,1024]{2,1,0:T(8,128)(2,1)} %wu_hbm.1, ...), custom_call_target="tpu_custom_call" | custom-call | tf_op jit(solution)/shard_map/pallas_call | solution.py:423
  81.9 1.6 %copy.11 = bf16[16,3584]{1,0:T(8,128)(2,1)} copy(bf16[16,3584]{1,0:T(8,128)(2,1)} %get-tuple-element.8) | data formatting | bytes 229376
  83.5 1.2 %copy.12 = bf16[16,8]{0,1:T(8,128)(2,1)} copy(bf16[16,8]{0,1:T(8,128)(2,1)} %bitcast.5) | data formatting | bytes 512

commit v3 on v2

v3 whole, which is shorter than its diff:
```python
import functools

import jax
import jax.numpy as jnp
from jax import lax
from jax.experimental import pallas as pl
from jax.experimental.pallas import tpu as pltpu
from jax.sharding import PartitionSpec as P

MESH = pl.DeviceIdType.MESH
BF = jnp.bfloat16
F32 = jnp.float32

ORDERS = (("x", "y", "z"), ("y", "z", "x"), ("z", "x", "y"))
HALF = 1792
WIDTHS = (640, 640, 512)
OFFS = (0, 640, 1280)
UNITS = ((0, 0), (0, 1), (0, 2), (1, 0), (1, 1), (1, 2))
BACK_W = {(0, 0): 256, (0, 1): 256, (0, 2): 256, (1, 0): 256, (1, 1): 384, (1, 2): 384}
BACK_OFF = {(0, 0): 0, (0, 1): 512, (0, 2): 1024, (1, 0): 1536, (1, 1): 2048, (1, 2): 2816}
BW = (256, 384)
STRIDE = {"z": 32, "y": 8, "x": 2}
SPLIT = {"z": 64, "y": 16, "x": 4}
NT = (((1,), (1,)), ((), ()))
TN = (((0,), (0,)), ((), ()))


def coords():
    node = lax.axis_index("node")
    local = lax.axis_index("local")
    return {"z": node // 4, "y": node % 4, "x": local // 2}, local % 2


def native_row(row, order):
    value = {a: (row // SPLIT[a]) % 4 for a in "xyz"}
    a1, a2, a3 = order
    return value[a3] * 64 + value[a2] * 16 + value[a1] * 4 + row % 4


def dot(a, b):
    return jnp.dot(a, b, preferred_element_type=F32)


def kernel(
    og, si, routes, gate_int, wg_hbm, wu_hbm, wd_hbm, out, gout,
    stage, b0, b1, b2, mown, mrecv, msum, ms, smat, kmask, sb0, sb1, sb2, gb, gr, xx, r1, r2,
    wg, wu, wd, pre, gg, gu, score, ysa, ysb, yra, yrb, zsa, zsb, zra, zrb, vsa, vsb, vra, vrb,
    wsem, ssem, snd, msnd, gsnd, rec1, rec2, rec3, rec4, mrec, mrec2, grec, rec5, rec6, rec7,
):
    pos, core = coords()
    bb, sb = (b0, b1, b2), (sb0, sb1, sb2)
    ys, yr, zs, zr, vs, vr = (ysa, ysb), (yra, yrb), (zsa, zsb), (zra, zrb), (vsa, vsb), (vra, vrb)
    KINDS = (1, 0)

    def at(axis, d, cc):
        p = dict(pos)
        p[axis] = (pos[axis] + d) % 4
        return (p["z"] * 4 + p["y"], p["x"] * 2 + (core + cc) % 2)

    def remote(src, dst, send, recv, axis, d, cc):
        return pltpu.make_async_remote_copy(
            src_ref=src, dst_ref=dst, send_sem=send, recv_sem=recv, device_id=at(axis, d, cc), device_id_type=MESH
        )

    def done(view, sem):
        pltpu.make_async_copy(view, view, sem).wait()

    def block(index, size):
        return pl.ds(pl.multiple_of(index * size, size), size)

    loads = [
        pltpu.make_async_copy(hbm.at[0], vmem, wsem.at[i])
        for i, (hbm, vmem) in enumerate(((wg_hbm, wg), (wu_hbm, wu), (wd_hbm, wd)))
    ]
    stages = [pltpu.make_async_copy(ref, stage.at[k], ssem.at[k]) for k, ref in enumerate((og, si))]
    for copy in stages + loads:
        copy.start()

    barrier = pltpu.get_barrier_semaphore()
    partners = [("x", 0, 1)] + [(a, d, cc) for a in "xyz" for d in (1, 2, 3) for cc in (0, 1)]
    for a, d, cc in partners:
        pl.semaphore_signal(barrier, inc=1, device_id=at(a, d, cc), device_id_type=MESH)

    gate_i = gate_int[...]
    table = jnp.concatenate([routes[...], gate_i // 256, gate_i % 256], axis=0).astype(F32).astype(BF)
    token = lax.broadcasted_iota(jnp.int32, (16, 128), 0)
    lane = lax.broadcasted_iota(jnp.int32, (16, 128), 1)
    for q, (a1, a2, a3) in enumerate(ORDERS):
        place = (lane == pos[a1] * 32 + core * 16 + token).astype(F32).astype(BF)
        laid = dot(table, place)
        mown[q, 0:8, :] = laid[0:8]
        mown[q, 8:16, :] = laid[8:16] * 256.0 + laid[16:24]

    for copy in stages:
        copy.wait()
    pl.semaphore_wait(barrier, len(partners))

    hops = [(d, cc) for d in (2, 1, 3, 0) for cc in (1, 0)]
    for k in KINDS:
        for q, (a1, a2, a3) in enumerate(ORDERS):
            dst = bb[q].at[k, pos[a2], block(pos[a1] * 2 + core, 16), :]
            for d, cc in hops:
                half = (core + cc) % 2
                src = stage.at[k, :, pl.ds(pl.multiple_of(half * HALF + OFFS[q], 128), WIDTHS[q])]
                if (d, cc) == (0, 0):
                    pltpu.make_async_copy(src, dst, rec1.at[k, q]).start()
                else:
                    remote(src, dst, snd.at[k, q], rec1.at[k, q], a1, d, cc).start()

    for q, (a1, a2, a3) in enumerate(ORDERS):
        for d, cc in hops:
            if (d, cc) != (0, 0):
                remote(mown.at[q], mrecv.at[q, pos[a1] * 2 + core], msnd.at[q], mrec.at[q], a1, d, cc).start()
        mrecv[q, pos[a1] * 2 + core] = mown[q]

    for k in KINDS:
        for q, (a1, a2, a3) in enumerate(ORDERS):
            done(bb[q].at[k, 0, pl.ds(0, 112), :], snd.at[k, q])
            done(bb[q].at[k, pos[a2]], rec1.at[k, q])
            mine = bb[q].at[k, pos[a2]]
            for d in (1, 3):
                remote(mine, mine, snd.at[k, q], rec2.at[k, q], a2, d, 0).start()

    for q, (a1, a2, a3) in enumerate(ORDERS):
        done(mrecv.at[q, pl.ds(0, 7)], msnd.at[q])
        done(mrecv.at[q, pl.ds(0, 7)], mrec.at[q])
        total = jnp.sum(mrecv[q], axis=0)
        msum[q] = total
        ms[q, pos[a2]] = total
        for d in (2, 1, 3):
            remote(msum.at[q], ms.at[q, pos[a2]], msnd.at[q], mrec2.at[q], a2, d, 0).start()

    for k in KINDS:
        for q, (a1, a2, a3) in enumerate(ORDERS):
            done(bb[q].at[k, pl.ds(0, 2)], snd.at[k, q])
            done(bb[q].at[k, pl.ds(0, 2)], rec2.at[k, q])
            for d, part in ((1, 0), (3, 1)):
                held = bb[q].at[k, (pos[a2] - d) % 4, pl.ds(part * 64, 64), :]
                remote(held, held, snd.at[k, q], rec3.at[k, q], a2, d, 0).start()

    up = lax.broadcasted_iota(jnp.int32, (256, 256), 0)
    across = lax.broadcasted_iota(jnp.int32, (256, 256), 1)
    earlier = ((up < across) & (up // 16 == across // 16)).astype(F32).astype(BF)
    lanes3 = lax.broadcasted_iota(jnp.int32, (8, 32, 128), 2).astype(F32)
    slots3 = lax.broadcasted_iota(jnp.int32, (8, 32, 256), 1).astype(F32)
    picks3 = lax.broadcasted_iota(jnp.int32, (8, 8, 256), 1).astype(F32)
    expert3 = lax.broadcasted_iota(jnp.int32, (8, 8, 256), 0)
    pair = ((lax.broadcasted_iota(jnp.int32, (8, 256), 1) // 16) * 2).astype(F32)

    def tables(q, p):
        a1, a2, a3 = ORDERS[q]
        base = pos[a1] * STRIDE[a1] + pos[a2] * STRIDE[a2]
        expert = ((expert3 // 2) * STRIDE[a3] + expert3 % 2 + base).astype(F32)
        meta = jnp.concatenate([ms[q, 2 * p], ms[q, 2 * p + 1]], axis=1)
        hit = jnp.where(meta[0:8][None] == expert, 1.0, 0.0)
        named = jnp.sum(hit, axis=1)
        rank = dot(named.astype(BF), earlier)
        code = jnp.where(named > 0.5, pair + rank, -1.0)
        chosen = jnp.where(code[:, None, :] == slots3, 1.0, 0.0)
        smat[q, p] = chosen.reshape(256, 256).astype(BF)
        if q == 0:
            gate = jnp.sum(hit * meta[8:16][None], axis=1)
            gate = jnp.sum(chosen * gate[:, None, :], axis=2, keepdims=True)
            gb[:, p * 32 : p * 32 + 32, :] = jnp.broadcast_to(gate * (1.0 / 65536.0), (8, 32, 128))
            pick = jnp.sum(hit * picks3, axis=1)
            pick = jnp.sum(chosen * pick[:, None, :], axis=2, keepdims=True)
            kmask[p] = jnp.where(lanes3 == pick, 1.0, 0.0).reshape(256, 128).astype(BF)

    for q, (a1, a2, a3) in enumerate(ORDERS):
        done(ms.at[q, pl.ds(0, 3)], msnd.at[q])
        done(ms.at[q, pl.ds(0, 3)], mrec2.at[q])
        for p in range(2):
            tables(q, p)

    for k in KINDS:
        for q, (a1, a2, a3) in enumerate(ORDERS):
            done(bb[q].at[k, 0], snd.at[k, q])
            done(bb[q].at[k, 0], rec3.at[k, q])
            for p in range(2):
                rows = dot(smat[q, p], bb[q][k, 2 * p : 2 * p + 2].reshape(256, WIDTHS[q]))
                sb[q][k, :, p * 32 : p * 32 + 32, :] = rows.astype(BF).reshape(8, 32, WIDTHS[q])
            there = block(pos[a3], 64)
            if q == 0:
                land = xx.at[k, there, pl.ds(pl.multiple_of(core * HALF, 128), WIDTHS[0])]
            else:
                land = (r1, r2)[q - 1].at[k, core, there, :]
            for d, cc in hops:
                src = sb[q].at[k, ((pos[a3] + d) % 4) * 2 + (core + cc) % 2]
                if (d, cc) == (0, 0):
                    pltpu.make_async_copy(src, land, rec4.at[k, q]).start()
                else:
                    remote(src, land, snd.at[k, q], rec4.at[k, q], a3, d, cc).start()

    gmine = gr.at[block(pos["z"], 64), :]
    for d in (2, 1, 3, 0):
        src = gb.at[((pos["z"] + d) % 4) * 2 + core]
        if d == 0:
            pltpu.make_async_copy(src, gmine, grec.at[0]).start()
        else:
            remote(src, gmine, gsnd.at[0], grec.at[0], "z", d, 0).start()

    iota_r = lax.broadcasted_iota(jnp.int32, (256, 256), 0)
    iota_c = lax.broadcasted_iota(jnp.int32, (256, 256), 1)

    def arrive(k):
        for q in range(3):
            done(sb[q].at[k, pl.ds(0, 7)], snd.at[k, q])
            done(sb[q].at[k], rec4.at[k, q])
            if q:
                perm = (native_row(iota_r, ORDERS[q]) == iota_c).astype(F32).astype(BF)
                for half in range(2):
                    start = half * HALF + OFFS[q]
                    rows = dot(perm, (r1, r2)[q - 1][k, half])
                    xx[k, :, start : start + WIDTHS[q]] = rows.astype(BF)

    arrive(1)
    for copy in loads:
        copy.wait()

    def forward(n, carry):
        at_n = block(n, 512)
        pre[0, :, at_n] = dot(xx[1], wg[:, at_n])
        pre[1, :, at_n] = dot(xx[1], wu[:, at_n])
        return carry

    lax.fori_loop(0, 2, forward, 0)
    arrive(0)
    score[...] = jnp.zeros_like(score)

    def backward(n, carry):
        at_n = block(n, 512)
        grad_hidden = lax.dot_general(xx[0], wd[at_n, :], NT, preferred_element_type=F32)
        pre_gate = pre[0, :, at_n]
        pre_up = pre[1, :, at_n]
        sig = jax.nn.sigmoid(pre_gate)
        act = pre_gate * sig
        grad_up = grad_hidden * act
        part = grad_up * pre_up
        score[...] += (part[:, 0:128] + part[:, 128:256]) + (part[:, 256:384] + part[:, 384:512])
        gu[:, at_n] = grad_up.astype(BF)
        gg[:, at_n] = (grad_hidden * pre_up * sig * (1.0 + pre_gate * (1.0 - sig))).astype(BF)
        return carry

    lax.fori_loop(0, 2, backward, 0)
    done(gr.at[pl.ds(0, 192), :], gsnd.at[0])
    done(gr, grec.at[0])

    def expert_rows(t, q):
        a1, a2, a3 = ORDERS[q]
        w = BACK_W[t, q]
        cols = pl.ds(BACK_OFF[t, q], 2 * w)
        rows = lax.dot_general(gg[...], wg[cols, :], NT, preferred_element_type=F32)
        rows = rows + lax.dot_general(gu[...], wu[cols, :], NT, preferred_element_type=F32)
        rows = (rows * gr[:, 0:1]).astype(BF)
        if q:
            back = (native_row(iota_c, ORDERS[q]) == iota_r).astype(F32).astype(BF)
            rows = dot(back, rows).astype(BF)
        for half in range(2):
            ys[t][q, half, :, 0:w] = rows[:, half * w : (half + 1) * w]
            if w < BW[t]:
                total = jnp.sum(score[...], axis=1, keepdims=True)
                ys[t][q, half, :, w : BW[t]] = jnp.broadcast_to(total, (256, 128)).astype(BF)
        mine = yr[t].at[q, pos[a3] * 2 + core]
        for d, cc in hops:
            src = ys[t].at[q, (core + cc) % 2, block((pos[a3] + d) % 4, 64), :]
            if (d, cc) == (0, 0):
                pltpu.make_async_copy(src, mine, rec5.at[t, q]).start()
            else:
                remote(src, mine, snd.at[t, q], rec5.at[t, q], a3, d, cc).start()

    def combine(t, q):
        a1, a2, a3 = ORDERS[q]
        done(yr[t].at[q, pl.ds(0, 7)], snd.at[t, q])
        done(yr[t].at[q], rec5.at[t, q])
        for p in range(2):
            got = yr[t][q, :, p * 32 : p * 32 + 32, :].reshape(256, BW[t])
            if BACK_W[t, q] < BW[t]:
                got = jnp.concatenate([got[:, 0:256], got[:, 256:384] * kmask[p]], axis=1)
            total = lax.dot_general(smat[q, p], got, TN, preferred_element_type=F32).astype(BF)
            zs[t][q, 2 * p : 2 * p + 2] = total.reshape(2, 128, BW[t])
        for d in (2, 1, 3, 0):
            src, dst = zs[t].at[q, (pos[a2] + d) % 4], zr[t].at[q, pos[a2]]
            if d == 0:
                pltpu.make_async_copy(src, dst, rec6.at[t, q]).start()
            else:
                remote(src, dst, snd.at[t, q], rec6.at[t, q], a2, d, 0).start()

    def narrow(t, q):
        a1, a2, a3 = ORDERS[q]
        done(zr[t].at[q, pl.ds(0, 3)], snd.at[t, q])
        done(zr[t].at[q], rec6.at[t, q])
        total = jnp.zeros((128, BW[t]), F32)
        for s in range(4):
            total = total + zr[t][q, s].astype(F32)
        vs[t][q] = total.astype(BF)
        dst = vr[t].at[q, core * 4 + pos[a1]]
        for d, cc in hops:
            src = vs[t].at[q, block(((pos[a1] + d) % 4) * 2 + (core + cc) % 2, 16), :]
            if (d, cc) == (0, 0):
                pltpu.make_async_copy(src, dst, rec7.at[t, q]).start()
            else:
                remote(src, dst, snd.at[t, q], rec7.at[t, q], a1, d, cc).start()

    def finish(t, q):
        done(vr[t].at[q, pl.ds(0, 7)], snd.at[t, q])
        done(vr[t].at[q], rec7.at[t, q])
        w = BACK_W[t, q]
        both = jnp.zeros((16, BW[t]), F32)
        for half in range(2):
            total = jnp.zeros((16, BW[t]), F32)
            for s in range(4):
                total = total + vr[t][q, half * 4 + s].astype(F32)
            start = BACK_OFF[t, q] + half * w
            out[:, start : start + w] = total[:, 0:w].astype(BF)
            both = both + total
        if w < BW[t]:
            same = lax.broadcasted_iota(jnp.int32, (16, 16), 0) == lax.broadcasted_iota(jnp.int32, (16, 16), 1)
            scores = (both[:, w : BW[t]] * 0.5).astype(BF)
            turned = lax.dot_general(scores, same.astype(F32).astype(BF), TN, preferred_element_type=F32)
            gout[...] = turned[0:8].astype(BF)

    for t, q in UNITS:
        expert_rows(t, q)
    for t, q in UNITS:
        combine(t, q)
    for t, q in UNITS:
        narrow(t, q)
    for t, q in UNITS:
        finish(t, q)


def shards(out_grad, saved_input, routes, gate_int, w_gate, w_up, w_down):
    vmem = pl.BlockSpec(memory_space=pltpu.VMEM)
    hbm = pl.BlockSpec(memory_space=pl.ANY)
    sem = pltpu.SemaphoreType.DMA
    scratch = (
        [pltpu.VMEM((2, 16, 3584), BF)]
        + [pltpu.VMEM((2, 4, 128, w), BF) for w in WIDTHS]
        + [
            pltpu.VMEM((3, 16, 128), F32),
            pltpu.VMEM((3, 8, 16, 128), F32),
            pltpu.VMEM((3, 16, 128), F32),
            pltpu.VMEM((3, 4, 16, 128), F32),
            pltpu.VMEM((3, 2, 256, 256), BF),
            pltpu.VMEM((2, 256, 128), BF),
        ]
        + [pltpu.VMEM((2, 8, 64, w), BF) for w in WIDTHS]
        + [
            pltpu.VMEM((8, 64, 128), F32),
            pltpu.VMEM((256, 128), F32),
            pltpu.VMEM((2, 256, 3584), BF),
            pltpu.VMEM((2, 2, 256, WIDTHS[1]), BF),
            pltpu.VMEM((2, 2, 256, WIDTHS[2]), BF),
            pltpu.VMEM((3584, 1024), BF),
            pltpu.VMEM((3584, 1024), BF),
            pltpu.VMEM((1024, 3584), BF),
            pltpu.VMEM((2, 256, 1024), F32),
            pltpu.VMEM((256, 1024), BF),
            pltpu.VMEM((256, 1024), BF),
            pltpu.VMEM((256, 128), F32),
        ]
        + [pltpu.VMEM((3, 2, 256, w), BF) for w in BW]
        + [pltpu.VMEM((3, 8, 64, w), BF) for w in BW]
        + [pltpu.VMEM((3, 4, 128, w), BF) for w in BW]
        + [pltpu.VMEM((3, 4, 128, w), BF) for w in BW]
        + [pltpu.VMEM((3, 128, w), BF) for w in BW]
        + [pltpu.VMEM((3, 8, 16, w), BF) for w in BW]
        + [sem((3,)), sem((2,)), sem((2, 3)), sem((3,)), sem((1,))]
        + [sem((2, 3))] * 4
        + [sem((3,)), sem((3,)), sem((1,))]
        + [sem((2, 3))] * 3
    )
    input_grad, gate_grad = pl.pallas_call(
        kernel,
        out_shape=(
            jax.ShapeDtypeStruct(out_grad.shape, BF),
            jax.ShapeDtypeStruct(routes.shape[::-1], BF),
        ),
        in_specs=[hbm, hbm, vmem, vmem, hbm, hbm, hbm],
        out_specs=(vmem, vmem),
        scratch_shapes=scratch,
        compiler_params=pltpu.CompilerParams(
            collective_id=0, has_side_effects=True, vmem_limit_bytes=64 * 2**20 - 65536
        ),
    )(out_grad, saved_input, routes.T, gate_int.T, w_gate, w_up, w_down)
    return input_grad, gate_grad.T


def solution(mesh):
    rows = P(("node", "local"), None)
    experts = P(("node", "local"), None, None)
    return jax.shard_map(
        shards,
        mesh=mesh,
        in_specs=(rows, rows, rows, rows, experts, experts, experts),
        out_specs=(rows, rows),
        check_vma=False,
    )
```

time: 84.9 us -> 77.5 us (0.913)
  Pallas kernels: 81.3 us -> 73.9 us
    pallas_call x1, Pallas kernels: 81.3 us -> 73.9 us  [shards(): pl.pallas_call(kernel, out_shape=(jax.ShapeDtypeStruct(out_grad.shape, BF...]
where the time goes in v3:
time: 77.5 us; the launch traced here: 77.3 us
  Pallas kernels  73.9 us (95%)
  local copies, waits for them, and re-layouts  2.8 us (4%)
    pallas_call x1, Pallas kernels, shards(): pl.pallas_call(kernel, out_shape=(jax.ShapeDtypeStruct(out_grad.shape, BF...  73.9 us
    unnamed x2, local copies, waits for them, and re-layouts  2.8 us

profile of v3, /device:TPU:1, one launch (start us, length us, event | category | flops | bytes accessed | tf_op | source)
XLA Modules:
  0.0 77.3 jit_solution(7794122175808168621)
XLA Ops:
  0.6 73.9 %shard_map.86 = (bf16[16,3584]{1,0:T(8,128)(2,1)}, bf16[8,16]{1,0:T(8,128)(2,1)}) custom-call(bf16[16,3584]{1,0:T(8,128)(2,1)} %og.1, bf16[16,3584]{1,0:T(8,128)(2,1)} %si.1, s32[8,16]{1,0:T(8,128)} %bitcast.3, s32[8,16]{1,0:T(8,128)} %bitcast.4, bf16[1,3584,1024]{2,1,0:T(8,128)(2,1)} %wg_hbm.1, bf16[1,3584,1024]{2,1,0:T(8,128)(2,1)} %wu_hbm.1, ...), custom_call_target="tpu_custom_call" | custom-call | tf_op jit(solution)/shard_map/pallas_call | solution.py:373
  74.5 1.6 %copy.11 = bf16[16,3584]{1,0:T(8,128)(2,1)} copy(bf16[16,3584]{1,0:T(8,128)(2,1)} %get-tuple-element.8) | data formatting | bytes 229376
  76.1 1.2 %copy.12 = bf16[16,8]{0,1:T(8,128)(2,1)} copy(bf16[16,8]{0,1:T(8,128)(2,1)} %bitcast.5) | data formatting | bytes 512

commit v4 on v3

--- a/solution.py
+++ b/solution.py
@@ -43,7 +43,7 @@
 
 def kernel(
     og, si, routes, gate_int, wg_hbm, wu_hbm, wd_hbm, out, gout,
-    stage, b0, b1, b2, mown, mrecv, msum, ms, smat, kmask, sb0, sb1, sb2, gb, gr, xx, r1, r2,
+    stage, b0, b1, b2, mown, mrecv, msum, ms, smat, turn, order, kmask, sb0, sb1, sb2, gb, gr, xx, r1, r2,
     wg, wu, wd, pre, gg, gu, score, ysa, ysb, yra, yrb, zsa, zsb, zra, zrb, vsa, vsb, vra, vrb,
     wsem, ssem, snd, msnd, gsnd, rec1, rec2, rec3, rec4, mrec, mrec2, grec, rec5, rec6, rec7,
 ):
@@ -73,7 +73,7 @@
         for i, (hbm, vmem) in enumerate(((wg_hbm, wg), (wu_hbm, wu), (wd_hbm, wd)))
     ]
     stages = [pltpu.make_async_copy(ref, stage.at[k], ssem.at[k]) for k, ref in enumerate((og, si))]
-    for copy in stages + loads:
+    for copy in stages:
         copy.start()
 
     barrier = pltpu.get_barrier_semaphore()
@@ -90,6 +90,12 @@
         laid = dot(table, place)
         mown[q, 0:8, :] = laid[0:8]
         mown[q, 8:16, :] = laid[8:16] * 256.0 + laid[16:24]
+
+    iota_r = lax.broadcasted_iota(jnp.int32, (256, 256), 0)
+    iota_c = lax.broadcasted_iota(jnp.int32, (256, 256), 1)
+    for q in (1, 2):
+        order[q - 1, 0] = (native_row(iota_r, ORDERS[q]) == iota_c).astype(F32).astype(BF)
+        order[q - 1, 1] = (native_row(iota_c, ORDERS[q]) == iota_r).astype(F32).astype(BF)
 
     for copy in stages:
         copy.wait()
@@ -121,6 +127,9 @@
             for d in (1, 3):
                 remote(mine, mine, snd.at[k, q], rec2.at[k, q], a2, d, 0).start()
 
+    for copy in loads:
+        copy.start()
+
     for q, (a1, a2, a3) in enumerate(ORDERS):
         done(mrecv.at[q, pl.ds(0, 7)], msnd.at[q])
         done(mrecv.at[q, pl.ds(0, 7)], mrec.at[q])
@@ -157,7 +166,9 @@
         rank = dot(named.astype(BF), earlier)
         code = jnp.where(named > 0.5, pair + rank, -1.0)
         chosen = jnp.where(code[:, None, :] == slots3, 1.0, 0.0)
-        smat[q, p] = chosen.reshape(256, 256).astype(BF)
+        chosen2 = chosen.reshape(256, 256)
+        smat[q, p] = chosen2.astype(BF)
+        turn[q, p] = chosen2.T.astype(BF)
         if q == 0:
             gate = jnp.sum(hit * meta[8:16][None], axis=1)
             gate = jnp.sum(chosen * gate[:, None, :], axis=2, keepdims=True)
@@ -199,18 +210,14 @@
         else:
             remote(src, gmine, gsnd.at[0], grec.at[0], "z", d, 0).start()
 
-    iota_r = lax.broadcasted_iota(jnp.int32, (256, 256), 0)
-    iota_c = lax.broadcasted_iota(jnp.int32, (256, 256), 1)
-
     def arrive(k):
         for q in range(3):
             done(sb[q].at[k, pl.ds(0, 7)], snd.at[k, q])
             done(sb[q].at[k], rec4.at[k, q])
             if q:
-                perm = (native_row(iota_r, ORDERS[q]) == iota_c).astype(F32).astype(BF)
                 for half in range(2):
                     start = half * HALF + OFFS[q]
-                    rows = dot(perm, (r1, r2)[q - 1][k, half])
+                    rows = dot(order[q - 1, 0], (r1, r2)[q - 1][k, half])
                     xx[k, :, start : start + WIDTHS[q]] = rows.astype(BF)
 
     arrive(1)
@@ -253,8 +260,7 @@
         rows = rows + lax.dot_general(gu[...], wu[cols, :], NT, preferred_element_type=F32)
         rows = (rows * gr[:, 0:1]).astype(BF)
         if q:
-            back = (native_row(iota_c, ORDERS[q]) == iota_r).astype(F32).astype(BF)
-            rows = dot(back, rows).astype(BF)
+            rows = dot(order[q - 1, 1], rows).astype(BF)
         for half in range(2):
             ys[t][q, half, :, 0:w] = rows[:, half * w : (half + 1) * w]
             if w < BW[t]:
@@ -276,7 +282,7 @@
             got = yr[t][q, :, p * 32 : p * 32 + 32, :].reshape(256, BW[t])
             if BACK_W[t, q] < BW[t]:
                 got = jnp.concatenate([got[:, 0:256], got[:, 256:384] * kmask[p]], axis=1)
-            total = lax.dot_general(smat[q, p], got, TN, preferred_element_type=F32).astype(BF)
+            total = dot(turn[q, p], got).astype(BF)
             zs[t][q, 2 * p : 2 * p + 2] = total.reshape(2, 128, BW[t])
         for d in (2, 1, 3, 0):
             src, dst = zs[t].at[q, (pos[a2] + d) % 4], zr[t].at[q, pos[a2]]
@@ -329,6 +335,11 @@
         finish(t, q)
 
 
+def hand_over(rows, scores, out, gout):
+    out[...] = rows[...]
+    gout[...] = scores[...]
+
+
 def shards(out_grad, saved_input, routes, gate_int, w_gate, w_up, w_down):
     vmem = pl.BlockSpec(memory_space=pltpu.VMEM)
     hbm = pl.BlockSpec(memory_space=pl.ANY)
@@ -342,6 +353,8 @@
             pltpu.VMEM((3, 16, 128), F32),
             pltpu.VMEM((3, 4, 16, 128), F32),
             pltpu.VMEM((3, 2, 256, 256), BF),
+            pltpu.VMEM((3, 2, 256, 256), BF),
+            pltpu.VMEM((2, 2, 256, 256), BF),
             pltpu.VMEM((2, 256, 128), BF),
         ]
         + [pltpu.VMEM((2, 8, 64, w), BF) for w in WIDTHS]
@@ -383,6 +396,15 @@
             collective_id=0, has_side_effects=True, vmem_limit_bytes=64 * 2**20 - 65536
         ),
     )(out_grad, saved_input, routes.T, gate_int.T, w_gate, w_up, w_down)
+    input_grad, gate_grad = pl.pallas_call(
+        hand_over,
+        out_shape=(
+            jax.ShapeDtypeStruct(out_grad.shape, BF),
+            jax.ShapeDtypeStruct(routes.shape[::-1], BF),
+        ),
+        in_specs=[vmem, vmem],
+        out_specs=(vmem, vmem),
+    )(input_grad, gate_grad)
     return input_grad, gate_grad.T
 
 

time: 77.5 us -> 74.1 us (0.956)
  local copies, waits for them, and re-layouts: 2.8 us -> 0 us
    unnamed x2 -> x0, local copies, waits for them, and re-layouts: 2.8 us -> none
    pallas_call x1, Pallas kernels: 73.9 us -> 71.7 us  [shards(): pl.pallas_call(kernel, out_shape=(jax.ShapeDtypeStruct(out_grad.shape, BF...]
    pallas_call x0 -> x1, Pallas kernels: none -> 1.56 us  [shards(): pl.pallas_call(hand_over, out_shape=(jax.ShapeDtypeStruct(out_grad.shape,...]
where the time goes in v4:
time: 74.1 us; the launch traced here: 73.9 us
  Pallas kernels  73.3 us (99%)
    pallas_call x1, Pallas kernels, shards(): pl.pallas_call(kernel, out_shape=(jax.ShapeDtypeStruct(out_grad.shape, BF...  71.7 us
    pallas_call x1, Pallas kernels, shards(): pl.pallas_call(hand_over, out_shape=(jax.ShapeDtypeStruct(out_grad.shape,...  1.56 us

profile of v4, /device:TPU:1, one launch (start us, length us, event | category | flops | bytes accessed | tf_op | source)
XLA Modules:
  0.0 73.9 jit_solution(7807001669167505591)
XLA Ops:
  0.6 71.7 %shard_map.86 = (bf16[16,3584]{1,0:T(8,128)(2,1)}, bf16[8,16]{1,0:T(8,128)(2,1)}) custom-call(bf16[16,3584]{1,0:T(8,128)(2,1)} %og.1, bf16[16,3584]{1,0:T(8,128)(2,1)} %si.1, s32[8,16]{1,0:T(8,128)} %bitcast.3, s32[8,16]{1,0:T(8,128)} %bitcast.4, bf16[1,3584,1024]{2,1,0:T(8,128)(2,1)} %wg_hbm.1, bf16[1,3584,1024]{2,1,0:T(8,128)(2,1)} %wu_hbm.1, ...), custom_call_target="tpu_custom_call" | custom-call | tf_op jit(solution)/shard_map/pallas_call | solution.py:386
  72.3 1.6 %shard_map.87 = (bf16[16,3584]{1,0:T(8,128)(2,1)}, bf16[8,16]{1,0:T(8,128)(2,1)}) custom-call(bf16[16,3584]{1,0:T(8,128)(2,1)} %get-tuple-element.6.rows, bf16[8,16]{1,0:T(8,128)(2,1)} %get-tuple-element.7.scores), custom_call_target="tpu_custom_call" | custom-call | tf_op jit(solution)/shard_map/pallas_call | solution.py:399
